TPU v7x, 512 devices: a whole 4x4x16 slice. The times are simulated.
512 devices in a mesh: seq: 64 (over z, y), ch: 8 (over x, core).
Axes of the slice: x: 4, y: 4, z: 16, core: 2. Of those that a mesh axis runs over, the one named last changes fastest.
Arguments:
- normalized_layer_entry: bfloat16 [8192, 4096], P('seq', 'ch'), may hold values from -6 to 6
- short_outer_query: bfloat16 [8192, 4096], P('seq', 'ch'), may hold values from -6 to 6
- short_inner_key: bfloat16 [8192, 4096], P('seq', 'ch'), may hold values from -6 to 6
- short_frozen_value: bfloat16 [8192, 4096], P('seq', 'ch'), may hold values from -6 to 6
- medium_outer_query: bfloat16 [8192, 4096], P('seq', 'ch'), may hold values from -6 to 6
- medium_inner_key: bfloat16 [8192, 4096], P('seq', 'ch'), may hold values from -6 to 6
- cotangent: bfloat16 [8192, 4096], P('seq', 'ch'), may hold values from -6 to 6
- adapter_down_factor: bfloat16 [64, 32, 4096], P('seq', None, 'ch'), may hold values from -0.09375 to 0.09375
- adapter_up_factor: bfloat16 [64, 32, 4096], P('seq', None, 'ch'), may hold values from -1 to 1
- token_clade: int32 [8192, 1], P('seq'), may hold values from 0 to 63; in each aligned block of 128 rows (0 to 127, 128 to 255, ...) at most 4 rows name the same one
- clade_storage_slot: int32 [64], replicated, may hold values from 0 to 63, each once
- short_group_filter: float32 [256, 7], P('ch'), may hold values from -2.4 to 2.4
- medium_undamped_filter: float32 [256, 128], P('ch'), may hold values from -0.6 to 0.6
- medium_decay_rate: float32 [256], P('ch'), may hold values from 0.003 to 0.06
Outputs:
- midrange_response: bfloat16 [8192, 4096], P('seq', 'ch')
- layer_entry_derivative: bfloat16 [8192, 4096], P('seq', 'ch')
- lowdim_projector_derivative: float32 [64, 32, 4096], P('seq', None, 'ch')
- lowdim_expander_derivative: float32 [64, 32, 4096], P('seq', None, 'ch')
- brief_convolution_derivative: float32 [256, 7], P('ch')
- midrange_raw_response_derivative: float32 [256, 128], P('ch')
Inputs may be any that keep to these rules, and one draw needn't show every extreme that they name: `token_clade`: among the 128 tokens of one device, no clade is named more than 4 times, a bound that some block reaches. `clade_storage_slot`: each slot holds exactly one clade's adapter.
All inputs are finite; a program needn't handle non-finite values.
Results may differ from a plain program's by a relative error of at most 0.012.
Values may be sent and summed in bfloat16 or wider, within the bound.
A program may use at most 64 MiB of HBM per device.

v0:
```python
import math

import jax
import jax.numpy as jnp
from jax import lax
from jax.sharding import PartitionSpec as P


def passed_along(value, axis, steps):
    count = lax.axis_size(axis)
    first, last = (max(0, -steps), min(count, count - steps))
    return lax.ppermute(value, axis, [(source, source + steps) for source in range(first, last)])


def band_matrix(kernel, out_len):
    groups, taps = kernel.shape
    full_len = out_len + taps - 1
    reversed_taps = kernel[:, ::-1]
    padded = jnp.concatenate(
        [reversed_taps, jnp.zeros((groups, full_len + 1 - taps), kernel.dtype)], axis=1
    )
    repeated_groups = jnp.tile(padded, (1, out_len))[:, : out_len * full_len]
    return repeated_groups.reshape(groups, out_len, full_len)


def causal_local(extended, kernel):
    groups, taps = kernel.shape
    full_len, feature_lanes = extended.shape
    out_len = full_len - taps + 1
    group_size = feature_lanes // groups
    per_block = math.gcd(groups, 8)
    blocks = groups // per_block
    shaped = extended.reshape(full_len, blocks, per_block, group_size).transpose(1, 2, 3, 0)
    kernel_blocks = kernel.reshape(blocks, per_block, taps)

    def one_block(pair):
        data, kern = pair
        band = band_matrix(kern, out_len)
        return jnp.einsum("gts,gcs->gct", band, data, precision=lax.Precision.HIGHEST)

    result = lax.map(one_block, (shaped, kernel_blocks))
    return result.transpose(3, 0, 1, 2).reshape(out_len, feature_lanes)


def to_slots(placing, values):
    return jnp.dot(placing, values, preferred_element_type=jnp.float32).astype(jnp.bfloat16)


def contract_last(left, right):
    return lax.dot_general(
        left, right, (((1,), (1,)), ((), ())), preferred_element_type=jnp.float32
    )


def contract_first(left, right):
    return lax.dot_general(
        left, right, (((0,), (0,)), ((), ())), preferred_element_type=jnp.float32
    )


def select_codes(products, owner_hot):
    sequence_length = products.shape[0]
    return jnp.sum(
        products.reshape(sequence_length, owner_hot.shape[1], -1) * owner_hot[:, :, None], axis=1
    )


def spread_codes(lineage_labels, owner_hot):
    sequence_length = lineage_labels.shape[0]
    return (
        (owner_hot[:, :, None] * lineage_labels.astype(jnp.float32)[:, None, :])
        .reshape(sequence_length, -1)
        .astype(jnp.bfloat16)
    )


def on_device(
    normalized_layer_entry,
    short_outer_query,
    short_inner_key,
    short_frozen_value,
    medium_outer_query,
    medium_inner_key,
    cotangent,
    adapter_down_factor,
    adapter_up_factor,
    token_clade,
    clade_storage_slot,
    short_group_filter,
    medium_undamped_filter,
    medium_decay_rate,
):
    sequence_length, feature_lanes = normalized_layer_entry.shape
    seq_count = lax.axis_size("seq")
    capacity = max(2, 2 * sequence_length // seq_count)
    slot_count = seq_count * capacity
    lowdim_breadth = adapter_down_factor.shape[1]
    short_len = short_group_filter.shape[1]
    medium_len = medium_undamped_filter.shape[1]
    group_size = feature_lanes // short_group_filter.shape[0]
    clade_hot = (
        token_clade[:, 0][:, None] == jnp.arange(seq_count, dtype=jnp.int32)[None, :]
    ).astype(jnp.float32)
    owner_token = jnp.sum(clade_hot * clade_storage_slot[None, :].astype(jnp.float32), axis=1)
    earlier_mask = (
        jnp.arange(sequence_length)[:, None] > jnp.arange(sequence_length)[None, :]
    ).astype(jnp.float32)
    earlier = jnp.dot(earlier_mask, clade_hot, precision=lax.Precision.HIGHEST)
    rank_inside = jnp.sum(clade_hot * earlier, axis=1)
    position = owner_token * capacity + rank_inside
    placing = (jnp.arange(slot_count, dtype=jnp.float32)[:, None] == position[None, :]).astype(
        jnp.bfloat16
    )
    owner_hot = (owner_token[:, None] == jnp.arange(seq_count, dtype=jnp.float32)[None, :]).astype(
        jnp.float32
    )
    all_down, all_up = (
        lax.all_gather(adapter_down_factor, "seq", axis=0, tiled=True),
        lax.all_gather(adapter_up_factor, "seq", axis=0, tiled=True),
    )
    flat_down = all_down.reshape(seq_count * lowdim_breadth, feature_lanes)
    flat_up = all_up.reshape(seq_count * lowdim_breadth, feature_lanes)
    lineage_labels = lax.psum(
        select_codes(contract_last(normalized_layer_entry, flat_down), owner_hot), "ch"
    ).astype(jnp.bfloat16)
    adapter_update = (
        0.5
        * jnp.dot(
            spread_codes(lineage_labels, owner_hot), flat_up, preferred_element_type=jnp.float32
        )
    ).astype(jnp.bfloat16)
    short_in = (
        short_inner_key.astype(jnp.float32)
        * (short_frozen_value.astype(jnp.float32) + adapter_update.astype(jnp.float32))
    ).astype(jnp.bfloat16)
    short_head = passed_along(short_in[sequence_length - (short_len - 1) :], "seq", 1)
    short_ext = jnp.concatenate([short_head, short_in], axis=0).astype(jnp.float32)
    taps_index = jnp.arange(medium_len, dtype=jnp.float32)
    decay_envelope = jnp.exp(-medium_decay_rate[:, None] * taps_index[None, :])
    medium_taps = medium_undamped_filter * decay_envelope
    short_conv, short_pull = jax.vjp(lambda kern: causal_local(short_ext, kern), short_group_filter)
    medium_operator_input = (
        medium_inner_key.astype(jnp.float32) * short_outer_query.astype(jnp.float32) * short_conv
    ).astype(jnp.bfloat16)
    medium_head = passed_along(
        medium_operator_input[sequence_length - (medium_len - 1) :], "seq", 1
    )
    medium_ext = jnp.concatenate([medium_head, medium_operator_input], axis=0).astype(jnp.float32)
    medium_conv, medium_pull = jax.vjp(lambda kern: causal_local(medium_ext, kern), medium_taps)
    midrange_response = (medium_outer_query.astype(jnp.float32) * medium_conv).astype(jnp.bfloat16)
    medium_gradient = (
        cotangent.astype(jnp.float32) * medium_outer_query.astype(jnp.float32)
    ).astype(jnp.bfloat16)
    (medium_tap_grad,) = medium_pull(medium_gradient.astype(jnp.float32))
    medium_next = passed_along(medium_gradient[: medium_len - 1], "seq", -1)
    medium_span = jnp.concatenate([medium_gradient, medium_next], axis=0).astype(jnp.float32)
    medium_in_grad = causal_local(medium_span[::-1], medium_taps)[::-1]
    short_grad = (
        medium_in_grad
        * medium_inner_key.astype(jnp.float32)
        * short_outer_query.astype(jnp.float32)
    ).astype(jnp.bfloat16)
    (short_tap_grad,) = short_pull(short_grad.astype(jnp.float32))
    short_next = passed_along(short_grad[: short_len - 1], "seq", -1)
    short_span = jnp.concatenate([short_grad, short_next], axis=0).astype(jnp.float32)
    short_in_grad = causal_local(short_span[::-1], short_group_filter)[::-1]
    short_total, medium_total = lax.psum((short_tap_grad, medium_tap_grad * decay_envelope), "seq")
    filter_gradient_scale = 1.0 / math.sqrt(sequence_length * seq_count * group_size)
    brief_convolution_derivative = short_total * filter_gradient_scale
    midrange_raw_response_derivative = medium_total * filter_gradient_scale
    correction_delta_derivative = (
        0.5 * short_in_grad * short_inner_key.astype(jnp.float32)
    ).astype(jnp.bfloat16)
    correction_multiplier = 1.0 / math.sqrt(sequence_length)
    lineage_labels_derivative = lax.psum(
        select_codes(contract_last(correction_delta_derivative, flat_up), owner_hot), "ch"
    ).astype(jnp.bfloat16)
    layer_entry_derivative = jnp.dot(
        spread_codes(lineage_labels_derivative, owner_hot),
        flat_down,
        preferred_element_type=jnp.float32,
    ).astype(jnp.bfloat16)
    packed = (
        to_slots(placing, normalized_layer_entry).reshape(seq_count, capacity, feature_lanes),
        to_slots(placing, lineage_labels).reshape(seq_count, capacity, lowdim_breadth),
        to_slots(placing, correction_delta_derivative).reshape(seq_count, capacity, feature_lanes),
        to_slots(placing, lineage_labels_derivative).reshape(seq_count, capacity, lowdim_breadth),
    )
    got_input, got_codes, got_delta, got_codes_grad = (
        lax.all_to_all(packed[0], "seq", split_axis=0, concat_axis=0, tiled=True),
        lax.all_to_all(packed[1], "seq", split_axis=0, concat_axis=0, tiled=True),
        lax.all_to_all(packed[2], "seq", split_axis=0, concat_axis=0, tiled=True),
        lax.all_to_all(packed[3], "seq", split_axis=0, concat_axis=0, tiled=True),
    )
    lowdim_expander_derivative = (
        contract_first(
            got_codes.reshape(slot_count, lowdim_breadth),
            got_delta.reshape(slot_count, feature_lanes),
        )
        * correction_multiplier
    )
    lowdim_projector_derivative = (
        contract_first(
            got_codes_grad.reshape(slot_count, lowdim_breadth),
            got_input.reshape(slot_count, feature_lanes),
        )
        * correction_multiplier
    )
    return (
        midrange_response,
        layer_entry_derivative,
        lowdim_projector_derivative.reshape(1, lowdim_breadth, feature_lanes),
        lowdim_expander_derivative.reshape(1, lowdim_breadth, feature_lanes),
        brief_convolution_derivative,
        midrange_raw_response_derivative,
    )


def solution(mesh):
    return jax.shard_map(
        on_device,
        mesh=mesh,
        in_specs=(
            P("seq", "ch"),
            P("seq", "ch"),
            P("seq", "ch"),
            P("seq", "ch"),
            P("seq", "ch"),
            P("seq", "ch"),
            P("seq", "ch"),
            P("seq", None, "ch"),
            P("seq", None, "ch"),
            P("seq", None),
            P(),
            P("ch", None),
            P("ch", None),
            P("ch"),
        ),
        out_specs=(
            P("seq", "ch"),
            P("seq", "ch"),
            P("seq", None, "ch"),
            P("seq", None, "ch"),
            P("ch", None),
            P("ch", None),
        ),
        check_vma=False,
    )
```

profile of v0, /device:TPU:2, one launch (start us, length us, event | category | flops | bytes accessed | tf_op | source)
XLA Modules:
  0.0 734.2 jit_solution(13968584702329256065)
XLA Ops:
  15.2 20.2 %all-to-all-start.1 = ((bf16[64,4,512]{2,1,0:T(4,128)(2,1)}), bf16[64,4,512]{2,1,0:T(4,128)(2,1)}, u32[]{:S(2)}, u32[]{:S(2)}) async-start(bf16[64,4,512]{2,1,0:T(4,128)(2,1)} %reshape.205), calls=%async_computation.1 | async-start | bytes 524288 | tf_op jit(solution)/shard_map/all_to_all | solution.py:190
  37.7 10.5 %while.70 = (s32[]{:T(128)}, f32[4,8,16,128]{3,2,1,0:T(8,128)S(1)}, f32[4,8,16,255]{3,2,1,0:T(8,128)S(1)}, f32[4,8,128]{2,1,0:T(8,128)S(1)}, s32[]{:T(128)}, /*index=5*/f32[]{:T(128)}) while((s32[]{:T(128)}, f32[4,8,16,128]{3,2,1,0:T(8,128)S(1)}, f32[4,8,16,255]{3,2,1,0:T(8,128)S(1)}, f32[4,8,128]{2,1,0:T(8,128)S(1)}, s32[]{:T(128)}, ...), condition=%wide.region_8.9_spmd, body=%wide.region_7.8_spmd.sunk | while | flops 50135040 | bytes 6509645 | solution.py:41
  51.8 3.2 collective-permute-done.3
  56.5 14.3 %while.71 = (s32[]{:T(128)}, f32[4,8,16,128]{3,2,1,0:T(8,128)}, f32[4,8,16,134]{3,2,1,0:T(8,128)S(1)}, f32[4,8,7]{2,1,0:T(8,128)S(1)}, s32[]{:T(128)}, /*index=5*/f32[]{:T(128)}) while((s32[]{:T(128)}, f32[4,8,16,128]{3,2,1,0:T(8,128)}, f32[4,8,16,134]{3,2,1,0:T(8,128)S(1)}, f32[4,8,7]{2,1,0:T(8,128)S(1)}, s32[]{:T(128)}, ...), condition=%wide.region_10.11_spmd, body=%wide.region_9.10_spmd.sunk | while | flops 26345472 | bytes 5110381 | solution.py:41
  74.1 83.2 %all-gather.5.cloned.1.call-done = bf16[64,32,512]{2,1,0:T(8,128)(2,1)} async-done(((bf16[1,32,512]{2,1,0:T(8,128)(2,1)}), bf16[64,32,512]{2,1,0:T(8,128)(2,1)}) %all-gather.5.cloned.1.call-update) | async-done | bytes 2097168 | tf_op jit(solution)/shard_map/all_gather | solution.py:119
  157.3 4.0 fusion.42
  161.3 135.9 %all-gather.3.cloned.1.call-done = bf16[64,32,512]{2,1,0:T(8,128)(2,1)} async-done(((bf16[1,32,512]{2,1,0:T(8,128)(2,1)}), bf16[64,32,512]{2,1,0:T(8,128)(2,1)}) %all-gather.3.cloned.1.call-update) | async-done | bytes 2097168 | tf_op jit(solution)/shard_map/all_gather | solution.py:118
  297.3 4.0 fusion.45
  301.3 20.7 %all-reduce.7 = (bf16[128,32]{0,1:T(8,128)(2,1)S(1)}, bf16[128,32]{0,1:T(8,128)(2,1)S(1)}) all-reduce(f32[128,32]{0,1:T(8,128)S(1)} %fusion.45, f32[128,32]{0,1:T(8,128)S(1)} %fusion.42), channel_id=1, replica_groups=mesh['seq'=64,'ch'=8] {'ch'}, use_global_device_ids=true, to_apply=%region_2.0 | all-reduce | flops 8192 | bytes 49152 | tf_op jit(solution)/shard_map/psum | solution.py:123
  322.0 4.2 fusion.72
  326.2 2.2 collective-permute-start
  328.7 3.1 fusion.69
  333.9 11.6 %all-to-all-start.3 = ((bf16[64,4,512]{2,1,0:T(4,128)(2,1)}), bf16[64,4,512]{2,1,0:T(4,128)(2,1)}, u32[]{:S(2)}, u32[]{:S(2)}) async-start(bf16[64,4,512]{2,1,0:T(4,128)(2,1)} %reshape.208), calls=%async_computation.3 | async-start | bytes 524288 | tf_op jit(solution)/shard_map/all_to_all | solution.py:192
  346.3 14.3 %while.68 = (s32[]{:T(128)}, f32[4,8,16,128]{3,2,1,0:T(8,128)}, f32[4,8,16,134]{3,2,1,0:T(8,128)S(1)}, f32[4,8,7]{2,1,0:T(8,128)S(1)}, s32[]{:T(128)}, /*index=5*/f32[]{:T(128)}) while((s32[]{:T(128)}, f32[4,8,16,128]{3,2,1,0:T(8,128)}, f32[4,8,16,134]{3,2,1,0:T(8,128)S(1)}, f32[4,8,7]{2,1,0:T(8,128)S(1)}, s32[]{:T(128)}, ...), condition=%wide.region_4.5_spmd, body=%wide.region_3.0_spmd.sunk | while | flops 26345472 | bytes 5110381 | solution.py:41
  364.1 4.0 collective-permute-start.1
  368.2 14.1 %all-to-all-start.2 = ((bf16[64,4,32]{2,1,0:T(4,128)(2,1)}), bf16[64,4,32]{2,1,0:T(4,128)(2,1)S(1)}, u32[]{:S(2)}, u32[]{:S(2)}) async-start(bf16[64,4,32]{2,1,0:T(4,128)(2,1)} %bitcast.49), calls=%async_computation.2 | async-start | bytes 131072 | tf_op jit(solution)/shard_map/all_to_all | solution.py:191
  382.8 14.1 %while.72 = (s32[]{:T(128)}, f32[4,8,7]{2,1,0:T(8,128)}, f32[4,8,16,128]{3,2,1,0:T(8,128)S(1)}, f32[4,8,16,134]{3,2,1,0:T(8,128)S(1)}, s32[]{:T(128)}, /*index=5*/s32[]{:T(128)}, f32[]{:T(128)}) while((s32[]{:T(128)}, f32[4,8,7]{2,1,0:T(8,128)}, f32[4,8,16,128]{3,2,1,0:T(8,128)S(1)}, f32[4,8,16,134]{3,2,1,0:T(8,128)S(1)}, s32[]{:T(128)}, ...), condition=%wide.region_16.17_spmd, body=%wide.region_14.16_spmd.sunk | while | flops 26482636 | bytes 4614565 | solution.py:41
  397.7 15.4 %all-to-all-start = ((bf16[64,4,32]{2,1,0:T(4,128)(2,1)}), bf16[64,4,32]{2,1,0:T(4,128)(2,1)S(1)}, u32[]{:S(2)}, u32[]{:S(2)}) async-start(bf16[64,4,32]{2,1,0:T(4,128)(2,1)} %bitcast.46), calls=%async_computation | async-start | bytes 131072 | tf_op jit(solution)/shard_map/all_to_all | solution.py:193
  413.1 1.8 fusion.78
  414.8 13.2 %all-to-all-done = bf16[64,4,32]{2,1,0:T(4,128)(2,1)S(1)} async-done(((bf16[64,4,32]{2,1,0:T(4,128)(2,1)}), bf16[64,4,32]{2,1,0:T(4,128)(2,1)S(1)}, u32[]{:S(2)}, u32[]{:S(2)}) %all-to-all-start) | async-done | bytes 16416 | tf_op jit(solution)/shard_map/all_to_all | solution.py:193
  428.0 1.8 fusion.76
  431.9 7.9 %while.73 = (s32[]{:T(128)}, f32[4,8,128]{2,1,0:T(8,128)S(1)}, f32[4,8,16,128]{3,2,1,0:T(8,128)S(1)}, f32[4,8,16,255]{3,2,1,0:T(8,128)S(1)}, s32[]{:T(128)}, /*index=5*/s32[]{:T(128)}, f32[]{:T(128)}) while((s32[]{:T(128)}, f32[4,8,128]{2,1,0:T(8,128)S(1)}, f32[4,8,16,128]{3,2,1,0:T(8,128)S(1)}, f32[4,8,16,255]{3,2,1,0:T(8,128)S(1)}, ...), condition=%wide.region_20.21_spmd, body=%wide.region_18.20_spmd.sunk | while | flops 50395136 | bytes 6505573 | solution.py:41
  439.8 275.1 %all-reduce.6 = (f32[32,7]{0,1:T(8,128)S(1)}, f32[32,128]{1,0:T(8,128)S(1)}) all-reduce(f32[32,7]{0,1:T(8,128)S(1)} %copy.96, f32[32,128]{1,0:T(8,128)S(1)} %bitcast_multiply_fusion), channel_id=1, replica_groups=mesh['seq'=64,'ch'=8] {'seq'}, use_global_device_ids=true, to_apply=%region_17.18 | all-reduce | flops 4320 | bytes 34560 | tf_op jit(solution)/shard_map/psum | solution.py:167
  716.1 10.5 %while.69 = (s32[]{:T(128)}, f32[4,8,16,128]{3,2,1,0:T(8,128)S(1)}, f32[4,8,16,255]{3,2,1,0:T(8,128)S(1)}, f32[4,8,128]{2,1,0:T(8,128)S(1)}, s32[]{:T(128)}, /*index=5*/f32[]{:T(128)}) while((s32[]{:T(128)}, f32[4,8,16,128]{3,2,1,0:T(8,128)S(1)}, f32[4,8,16,255]{3,2,1,0:T(8,128)S(1)}, f32[4,8,128]{2,1,0:T(8,128)S(1)}, s32[]{:T(128)}, ...), condition=%wide.region_6.7_spmd, body=%wide.region_5.6_spmd.sunk | while | flops 50135040 | bytes 6509645 | solution.py:41
  (275 shorter events, 101.2 us)
Async XLA Ops:
  7.2 7.0 copy-start
  7.2 28.9 %copy-start.12 = (f32[32]{0:T(128)S(1)}, f32[32]{0:T(128)}, u32[]{:S(2)}) copy-start(f32[32]{0:T(128)} %param.39) | copy-start | bytes 388
  7.2 29.0 %copy-start.3 = (f32[32,128]{1,0:T(8,128)S(1)}, f32[32,128]{1,0:T(8,128)}, u32[]{:S(2)}) copy-start(f32[32,128]{1,0:T(8,128)} %param.38) | copy-start | bytes 49156
  7.2 150.0 %all-gather.5.cloned.1.call-start = ((), (), s32[]{:S(2)}) async-start(), calls=%async_computation.5 | async-start | bytes 2129920 | tf_op jit(solution)/shard_map/all_gather | solution.py:119
  10.0 26.6 %collective-permute-start.2 = (bf16[127,512]{0,1:T(8,128)(2,1)S(1)}, bf16[127,512]{0,1:T(8,128)(2,1)S(1)}, u32[]{:S(2)}, u32[]{:S(2)}) collective-permute-start(bf16[127,512]{0,1:T(8,128)(2,1)S(1)} %bitcast.204), channel_id=1, source_target_pairs={{8,0},{16,8},{24,16},{32,24},{40,32},{48,40},{56,48},{64,56},{72,6... | collective-permute-start | bytes 390152 | tf_op jit(solution)/shard_map/ppermute | solution.py:12
  13.7 0.5 copy-start.9
  14.2 21.2 %copy-start.7 = (f32[128]{0:T(128)}, f32[128]{0:T(128)S(1)}, u32[]{:S(2)}) copy-start(f32[128]{0:T(128)S(1)} %multiply_add_fusion) | copy-start | bytes 1540
  15.2 318.7 %all-to-all-start.1 = ((bf16[64,4,512]{2,1,0:T(4,128)(2,1)}), bf16[64,4,512]{2,1,0:T(4,128)(2,1)}, u32[]{:S(2)}, u32[]{:S(2)}) async-start(bf16[64,4,512]{2,1,0:T(4,128)(2,1)} %reshape.205), calls=%async_computation.1 | async-start | bytes 524288 | tf_op jit(solution)/shard_map/all_to_all | solution.py:190
  35.4 261.9 %all-gather.3.cloned.1.call-start = ((), (), s32[]{:S(2)}) async-start(), calls=%async_computation.4 | async-start | bytes 2129920 | tf_op jit(solution)/shard_map/all_gather | solution.py:118
  36.1 0.5 copy-start.5
  37.7 10.8 %copy-start.1 = (bf16[128,512]{1,0:T(8,128)(2,1)S(1)}, bf16[128,512]{1,0:T(8,128)(2,1)}, u32[]{:S(2)}) copy-start(bf16[128,512]{1,0:T(8,128)(2,1)} %param.27) | copy-start | bytes 393220
  37.7 13.9 %copy-start.4 = (f32[32,7]{0,1:T(8,128)S(1)}, f32[32,7]{0,1:T(8,128)}, u32[]{:S(2)}) copy-start(f32[32,7]{0,1:T(8,128)} %param.37) | copy-start | bytes 2692
  49.4 5.5 collective-permute-start.3
  56.5 15.6 %copy-start.8 = (f32[128]{0:T(128)S(1)}, f32[128]{0:T(128)}, u32[]{:S(2)}) copy-start(f32[128]{0:T(128)} %copy-done.7) | copy-start | bytes 1540
  70.8 86.4 %copy-start.2 = (bf16[128,512]{1,0:T(8,128)(2,1)S(1)}, bf16[128,512]{1,0:T(8,128)(2,1)}, u32[]{:S(2)}) copy-start(bf16[128,512]{1,0:T(8,128)(2,1)} %param.28) | copy-start | bytes 393220
  161.3 160.7 %copy-start.11 = (bf16[128,512]{1,0:T(8,128)(2,1)S(1)}, bf16[128,512]{1,0:T(8,128)(2,1)}, u32[]{:S(2)}) copy-start(bf16[128,512]{1,0:T(8,128)(2,1)} %param.29) | copy-start | bytes 393220
  322.0 6.6 copy-start.10
  326.2 7.3 collective-permute-start
  333.9 34.3 %all-to-all-start.3 = ((bf16[64,4,512]{2,1,0:T(4,128)(2,1)}), bf16[64,4,512]{2,1,0:T(4,128)(2,1)}, u32[]{:S(2)}, u32[]{:S(2)}) async-start(bf16[64,4,512]{2,1,0:T(4,128)(2,1)} %reshape.208), calls=%async_computation.3 | async-start | bytes 524288 | tf_op jit(solution)/shard_map/all_to_all | solution.py:192
  364.1 65.6 %collective-permute-start.1 = (bf16[127,512]{1,0:T(8,128)(2,1)}, bf16[127,512]{1,0:T(8,128)(2,1)}, u32[]{:S(2)}, u32[]{:S(2)}) collective-permute-start(bf16[127,512]{1,0:T(8,128)(2,1)} %slice.33), channel_id=1, source_target_pairs={{0,8},{8,16},{16,24},{24,32},{32,40},{40,48},{48,56},{56,64},{64,7... | collective-permute-start | bytes 390152 | tf_op jit(solution)/shard_map/ppermute | solution.py:12
  368.2 29.5 %all-to-all-start.2 = ((bf16[64,4,32]{2,1,0:T(4,128)(2,1)}), bf16[64,4,32]{2,1,0:T(4,128)(2,1)S(1)}, u32[]{:S(2)}, u32[]{:S(2)}) async-start(bf16[64,4,32]{2,1,0:T(4,128)(2,1)} %bitcast.49), calls=%async_computation.2 | async-start | bytes 131072 | tf_op jit(solution)/shard_map/all_to_all | solution.py:191
  397.7 30.3 %all-to-all-start = ((bf16[64,4,32]{2,1,0:T(4,128)(2,1)}), bf16[64,4,32]{2,1,0:T(4,128)(2,1)S(1)}, u32[]{:S(2)}, u32[]{:S(2)}) async-start(bf16[64,4,32]{2,1,0:T(4,128)(2,1)} %bitcast.46), calls=%async_computation | async-start | bytes 131072 | tf_op jit(solution)/shard_map/all_to_all | solution.py:193
  431.8 7.9 %copy-start.6 = (f32[32]{0:T(128)S(1)}, f32[32]{0:T(128)}, u32[]{:S(2)}) copy-start(f32[32]{0:T(128)} %copy-done.5) | copy-start | bytes 388
Sparse Core Ops, SparseCore 0:
  11.0 146.2 all-gather.4
  160.2 137.0 all-gather.2
where the time goes:
time: 735 us; the launch traced here: 734 us
  blocking collectives  296 us (40%)
  waiting for transfers between devices  237 us (32%)
  starting transfers between devices  70.3 us (10%)
  local copies, waits for them, and re-layouts  58.2 us (8%)
  matrix products  50 us (7%)
  between operations  14.5 us (2%)
  other arithmetic  7.68 us (1%)
    psum x1, blocking collectives, on_device(): lax.psum((short_tap_grad, medium_tap_grad * decay_envelope), 'seq')  275 us
    all_gather x1, waiting for transfers between devices, on_device(): lax.all_gather(adapter_down_factor, 'seq', axis=0, tiled=True)  136 us
    all_gather x1, waiting for transfers between devices, on_device(): lax.all_gather(adapter_up_factor, 'seq', axis=0, tiled=True)  83.2 us
    dot_general x24, matrix products, one_block(): jnp.einsum('gts,gcs->gct', band, data, precision=lax.Precision.HIGHEST)  28.5 us
    reshape x24, local copies, waits for them, and re-layouts, band_matrix(): return repeated_groups.reshape(groups, out_len, full_len)  25.7 us
    psum x1, blocking collectives, on_device(): lax.psum(select_codes(contract_last(normalized_layer_entry, flat_down), o...  20.7 us
    all_to_all x1, starting transfers between devices, on_device(): lax.all_to_all(packed[0], 'seq', split_axis=0, concat_axis=0, tiled=True)  20.2 us
    all_to_all x1, starting transfers between devices, on_device(): lax.all_to_all(packed[3], 'seq', split_axis=0, concat_axis=0, tiled=True)  15.4 us
  transfers between devices with their start and end apart: 10, of which 4 were waited for; matrix products, arithmetic and copies ran while one was open for 13% of the time, Pallas kernels for 0%

commit v1 on v0

v1 whole, which is shorter than its diff:
```python
import functools
import math

import jax
import jax.numpy as jnp
from jax import lax
from jax.experimental import pallas as pl
from jax.experimental.pallas import tpu as pltpu
from jax.sharding import PartitionSpec as P

F32, BF16 = jnp.float32, jnp.bfloat16
MESH = pl.DeviceIdType.MESH
LANES = 128
(MG_HALO, SG_HALO, SI_HALO, MED_HALO, X_OUT, DG_OUT, DELTA_BACK, DX_BACK, CODES, CODES_GRAD, SUM_Y, SUM_Z, SPREAD_Y) = range(13)


def mm(left, right):
    return jnp.dot(left, right, preferred_element_type=F32)


def mm_t(left, right, precision=None):
    return lax.dot_general(
        left, right, (((1,), (1,)), ((), ())), precision=precision, preferred_element_type=F32
    )


def t_mm(left, right, precision=None):
    return lax.dot_general(
        left, right, (((0,), (0,)), ((), ())), precision=precision, preferred_element_type=F32
    )


def iota(shape, axis):
    return lax.broadcasted_iota(jnp.int32, shape, axis)


def lane_block(index):
    return pl.ds(pl.multiple_of(index * LANES, LANES), LANES)


def stacked(value):
    return jnp.concatenate(
        [value[:, b * LANES : (b + 1) * LANES] for b in range(value.shape[1] // LANES)], axis=0
    )


def kernel(
    n_seq, n_ch, n_y, cap,
    x, soq, sik, sfv, moq, mik, cot, down, up, clade, storage, short_filter, medium_filter, rate,
    response, dx_out, projector, expander, brief, midrange,
    place, place_t, swap, toep_b, toep_f, mgext, sgext, siext, medext,
    xs, xr, ds, dr, us, ur, es, er, yx, yd, codes_all, cgrad_all, fg, yr, zr, fr, taps, mirror,
    send, recv,
):
    tokens, width = x.shape
    blocks = width // LANES
    slots = n_seq * cap
    chunk = blocks * cap
    groups = short_filter.shape[0]
    short_len = short_filter.shape[1]
    per_block = groups // blocks
    size = width // groups
    n_z = n_seq // n_y
    me, mine = lax.axis_index("seq"), lax.axis_index("ch")
    my_z, my_y = me // n_y, lax.rem(me, n_y)

    def push(kind, source, target, device):
        pltpu.make_async_remote_copy(
            src_ref=source, dst_ref=target, send_sem=send.at[kind], recv_sem=recv.at[kind],
            device_id=device, device_id_type=MESH,
        ).start()

    def landed(kind, ref):
        pltpu.make_async_copy(ref, ref, recv.at[kind]).wait()

    def gone(kind, ref):
        pltpu.make_async_copy(ref, ref, send.at[kind]).wait()

    def rows_of(ref, device):
        return ref.at[pl.ds(pl.multiple_of(device * chunk, chunk), chunk), :]

    def exchange(kind, source, target):
        @pl.loop(1, n_seq)
        def _(step):
            peer = lax.rem(me + step, n_seq)
            push(kind, rows_of(source, peer), rows_of(target, me), {"seq": peer})

        pltpu.make_async_copy(rows_of(source, me), rows_of(target, me), recv.at[kind]).start()

    def share(kind, ref):
        @pl.loop(1, n_ch)
        def _(step):
            peer = lax.rem(mine + step, n_ch)
            push(kind, ref.at[mine], ref.at[mine], {"ch": peer})

    barrier = pltpu.get_barrier_semaphore()

    @pl.loop(1, n_seq)
    def _(step):
        pl.semaphore_signal(
            barrier, inc=1, device_id={"seq": lax.rem(me + step, n_seq)}, device_id_type=MESH
        )

    @pl.loop(1, n_ch)
    def _(step):
        pl.semaphore_signal(
            barrier, inc=1, device_id={"ch": lax.rem(mine + step, n_ch)}, device_id_type=MESH
        )

    square = (tokens, tokens)
    eye = iota(square, 0) == iota(square, 1)
    clade_row = jnp.sum(jnp.where(eye, clade[...], 0).astype(F32), axis=0, keepdims=True)
    clade_col = clade[...].astype(F32)
    earlier = (clade_col == clade_row) & (iota(square, 1) < iota(square, 0))
    rank = jnp.sum(jnp.where(earlier, 1.0, 0.0), axis=1, keepdims=True)
    names = iota((tokens, n_seq), 1).astype(F32)
    owner = jnp.sum(
        jnp.where(clade_col == names, storage[...].astype(F32), 0.0), axis=1, keepdims=True
    )
    key_col = owner * chunk + rank
    key_row = jnp.sum(jnp.where(eye, key_col, 0.0), axis=0, keepdims=True).astype(jnp.int32)
    key_col = key_col.astype(jnp.int32)
    for b in range(blocks):
        lanes = slice(b * LANES, (b + 1) * LANES)
        place[:, lanes] = jnp.where(
            iota((slots * blocks, tokens), 0) == key_row + b * cap, 1.0, 0.0
        ).astype(BF16)
    xs[...] = mm(place[...], stacked(x[...])).astype(BF16)
    mgext[0:tokens, :] = (cot[...].astype(F32) * moq[...].astype(F32)).astype(BF16)

    pl.semaphore_wait(barrier, n_seq - 1 + n_ch - 1)

    @pl.when(me > 0)
    def _():
        push(MG_HALO, mgext.at[0:tokens, :], mgext.at[tokens : 2 * tokens, :], {"seq": me - 1})

    exchange(X_OUT, xs, xr)

    eye_g = iota((groups, groups), 0) == iota((groups, groups), 1)
    rate_col = jnp.sum(jnp.where(eye_g, rate[...], 0.0), axis=1, keepdims=True)
    envelope = jnp.exp(-rate_col * iota((groups, LANES), 1).astype(F32))
    damped = medium_filter[...] * envelope
    turned = jnp.where(
        iota(square, 0) == lax.rem(tokens - iota(square, 1), tokens), 1.0, 0.0
    ).astype(BF16)
    taps[...] = damped
    mirror[...] = mm(damped.astype(BF16), turned)
    row, col = iota(square, 0), iota(square, 1)

    @pl.loop(0, groups)
    def _(g):
        for source, target, own in ((taps, toep_b, col >= row), (mirror, toep_f, col <= row)):
            wide = jnp.broadcast_to(source[pl.ds(g, 1), :], square)
            band = pltpu.roll(wide, 0, 1, stride=1, stride_axis=0)
            target[g, :, 0:tokens] = jnp.where(own, band, 0.0).astype(BF16)
            target[g, :, tokens : 2 * tokens] = jnp.where(own, 0.0, band).astype(BF16)

    of_group = jnp.where(
        iota((groups, width), 1) // size == iota((groups, width), 0), 1.0, 0.0
    )
    short_wide = t_mm(short_filter[...], of_group, lax.Precision.HIGHEST)
    lane_group = iota(square, 1) // size

    def banded(ref, bands, b):
        data = ref[:, lane_block(b)]
        total = jnp.zeros(square, F32)
        for q in range(per_block):
            total = jnp.where(lane_group == q, mm(bands[b * per_block + q], data), total)
        return total

    @pl.when(me < n_seq - 1)
    def _():
        landed(MG_HALO, mgext.at[tokens : 2 * tokens, :])

    @pl.when(me == n_seq - 1)
    def _():
        mgext[tokens : 2 * tokens, :] = jnp.zeros((tokens, width), BF16)

    @pl.loop(0, blocks)
    def _(b):
        lanes = lane_block(b)
        gates = mik[:, lanes].astype(F32) * soq[:, lanes].astype(F32)
        sgext[0:tokens, lanes] = (banded(mgext, toep_b, b) * gates).astype(BF16)

    @pl.when(me > 0)
    def _():
        push(SG_HALO, sgext.at[0:16, :], sgext.at[tokens : tokens + 16, :], {"seq": me - 1})

    part = 2 * LANES
    per_part = part // blocks
    at = iota((part, part), 0)
    inside = lax.rem(at, per_part)
    wanted = (inside // cap) * chunk + (at // per_part) * cap + lax.rem(inside, cap)
    swap[...] = jnp.where(iota((part, part), 1) == wanted, 1.0, 0.0).astype(BF16)

    def opened(packed, target):
        for p in range(slots // per_part):
            turned_rows = mm(swap[...], packed[p * part : (p + 1) * part, :]).astype(BF16)
            for b in range(blocks):
                target[p * per_part : (p + 1) * per_part, b * LANES : (b + 1) * LANES] = (
                    turned_rows[b * per_part : (b + 1) * per_part]
                )

    def closed(value, packed):
        for p in range(slots // per_part):
            piece = stacked(value[p * per_part : (p + 1) * per_part])
            packed[p * part : (p + 1) * part, :] = t_mm(swap[...], piece).astype(BF16)

    landed(X_OUT, xr)
    opened(xr, yx)
    codes_all[mine] = mm_t(down[0], yx[...])
    share(CODES, codes_all)

    @pl.when(me < n_seq - 1)
    def _():
        landed(SG_HALO, sgext.at[tokens : tokens + 16, :])

    @pl.when(me == n_seq - 1)
    def _():
        sgext[tokens : tokens + 16, :] = jnp.zeros((16, width), BF16)

    ahead = sgext[...].astype(F32)
    total = jnp.zeros((tokens, width), F32)
    for j in range(short_len):
        total = total + short_wide[j : j + 1, :] * ahead[j : j + tokens]
    delta_grad = (0.5 * total * sik[...].astype(F32)).astype(BF16)
    ds[...] = mm(place[...], stacked(delta_grad)).astype(BF16)
    exchange(DG_OUT, ds, dr)

    def summed(ref):
        total = ref[0]
        for c in range(1, ref.shape[0]):
            total = total + ref[c]
        return total

    landed(CODES, codes_all.at[0 : n_ch - 1])
    codes = summed(codes_all).astype(BF16)
    closed((0.5 * t_mm(codes, up[0])).astype(BF16), us)
    exchange(DELTA_BACK, us, ur)

    for b in range(blocks):
        place_t[b * tokens : (b + 1) * tokens, :] = jnp.where(
            iota((tokens, slots * blocks), 1) == key_col + b * cap, 1.0, 0.0
        ).astype(BF16)

    weight_scale = 1.0 / math.sqrt(tokens)
    landed(DG_OUT, dr)
    opened(dr, yd)
    cgrad_all[mine] = mm_t(up[0], yd[...])
    share(CODES_GRAD, cgrad_all)
    expander[0] = mm(codes, yd[...]) * weight_scale

    landed(DELTA_BACK, ur)
    delta = mm(place_t[...], ur[...]).astype(BF16).astype(F32)
    for b in range(blocks):
        lanes = slice(b * LANES, (b + 1) * LANES)
        siext[16 : 16 + tokens, lanes] = (
            sik[:, lanes].astype(F32)
            * (sfv[:, lanes].astype(F32) + delta[b * tokens : (b + 1) * tokens])
        ).astype(BF16)

    @pl.when(me < n_seq - 1)
    def _():
        push(SI_HALO, siext.at[tokens : tokens + 16, :], siext.at[0:16, :], {"seq": me + 1})

    landed(CODES_GRAD, cgrad_all.at[0 : n_ch - 1])
    codes_grad = summed(cgrad_all).astype(BF16)
    closed(t_mm(codes_grad, down[0]).astype(BF16), es)
    exchange(DX_BACK, es, er)

    @pl.when(me > 0)
    def _():
        landed(SI_HALO, siext.at[0:16, :])

    @pl.when(me == 0)
    def _():
        siext[0:16, :] = jnp.zeros((16, width), BF16)

    behind = siext[...].astype(F32)
    total = jnp.zeros((tokens, width), F32)
    for j in range(short_len):
        total = total + short_wide[j : j + 1, :] * behind[16 - j : 16 - j + tokens]
    medext[0:tokens, :] = (mik[...].astype(F32) * soq[...].astype(F32) * total).astype(BF16)

    @pl.when(me < n_seq - 1)
    def _():
        push(MED_HALO, medext.at[0:tokens, :], medext.at[tokens : 2 * tokens, :], {"seq": me + 1})

    projector[0] = mm(codes_grad, yx[...]) * weight_scale
    short_grad = sgext[0:tokens, :].astype(F32)
    fg[:, 8:16, :] = jnp.zeros((blocks, 8, LANES), F32)
    for j in range(short_len):
        line = jnp.sum(short_grad * behind[16 - j : 16 - j + tokens], axis=0, keepdims=True)
        for b in range(blocks):
            fg[b, 8 + j : 9 + j, :] = line[:, b * LANES : (b + 1) * LANES]

    @pl.when(me > 0)
    def _():
        landed(MED_HALO, medext.at[tokens : 2 * tokens, :])

    @pl.when(me == 0)
    def _():
        medext[tokens : 2 * tokens, :] = jnp.zeros((tokens, width), BF16)

    flip = jnp.where(row + col == tokens - 1, 1.0, 0.0).astype(BF16)

    @pl.loop(0, blocks)
    def _(b):
        lanes = lane_block(b)
        grads = mgext[0:tokens, lanes].astype(F32)
        data = jnp.concatenate(
            [
                mm(flip, medext[0:tokens, lanes]).astype(BF16),
                mm(flip, medext[tokens : 2 * tokens, lanes]).astype(BF16),
            ],
            axis=0,
        )
        for q in range(per_block):
            masked = jnp.where(lane_group == q, grads, 0.0).astype(BF16)
            product = mm_t(masked, data)
            merged = jnp.where(
                col + row >= tokens - 1, product[:, 0:tokens], product[:, tokens : 2 * tokens]
            )
            lined = pltpu.roll(merged, 1, 1, stride=1, stride_axis=0)
            fg[b, q : q + 1, :] = jnp.sum(lined, axis=0, keepdims=True)

    yr[my_y] = fg[my_y]

    @pl.loop(1, n_y)
    def _(step):
        peer = lax.rem(my_y + step, n_y)
        push(SUM_Y, fg.at[peer], yr.at[my_y], {"seq": my_z * n_y + peer})

    def respond(b):
        lanes = lane_block(b)
        response[:, lanes] = (
            banded(medext, toep_f, b) * moq[:, lanes].astype(F32)
        ).astype(BF16)

    @pl.loop(0, blocks // 2)
    def _(b):
        respond(b)

    landed(SUM_Y, yr.at[0 : n_y - 1])
    zr[my_z] = summed(yr)

    @pl.loop(1, n_z)
    def _(step):
        peer = lax.rem(my_z + step, n_z)
        push(SUM_Z, zr.at[my_z], zr.at[my_z], {"seq": peer * n_y + my_y})

    @pl.loop(blocks // 2, blocks)
    def _(b):
        respond(b)

    landed(DX_BACK, er)
    back = mm(place_t[...], er[...]).astype(BF16)
    for b in range(blocks):
        dx_out[:, b * LANES : (b + 1) * LANES] = back[b * tokens : (b + 1) * tokens]

    landed(SUM_Z, zr.at[0 : n_z - 1])
    fr[my_y] = summed(zr)

    @pl.loop(1, n_y)
    def _(step):
        peer = lax.rem(my_y + step, n_y)
        push(SPREAD_Y, fr.at[my_y], fr.at[my_y], {"seq": my_z * n_y + peer})

    @pl.when(me > 0)
    def _():
        gone(MG_HALO, mgext.at[0:tokens, :])
        gone(SG_HALO, sgext.at[0:16, :])

    @pl.when(me < n_seq - 1)
    def _():
        gone(SI_HALO, siext.at[tokens : tokens + 16, :])
        gone(MED_HALO, medext.at[0:tokens, :])

    for kind, ref in ((X_OUT, xs), (DG_OUT, ds), (DELTA_BACK, us), (DX_BACK, es)):
        gone(kind, ref.at[0 : (n_seq - 1) * chunk, :])
    gone(CODES, codes_all.at[0 : n_ch - 1])
    gone(CODES_GRAD, cgrad_all.at[0 : n_ch - 1])
    gone(SUM_Y, fg.at[0 : n_y - 1])
    gone(SUM_Z, zr.at[0 : n_z - 1])

    landed(SPREAD_Y, fr.at[0 : n_y - 1])
    gone(SPREAD_Y, fr.at[0 : n_y - 1])
    filter_scale = 1.0 / math.sqrt(tokens * n_seq * size)
    for b in range(blocks):
        rows = slice(b * per_block, (b + 1) * per_block)
        midrange[rows, :] = fr[b, 0:8, :] * (envelope[rows] * filter_scale)
    lines = jnp.concatenate([fr[b, 8:16, :] for b in range(blocks)], axis=1)
    brief[...] = mm_t(of_group, lines, lax.Precision.HIGHEST)[:, 0:short_len] * filter_scale


def on_device(n_y, *arguments):
    x, down, storage = arguments[0], arguments[7], arguments[10]
    short_filter, medium_filter = arguments[11], arguments[12]
    tokens, width = x.shape
    n_seq, n_ch = lax.axis_size("seq"), lax.axis_size("ch")
    cap = max(2, 2 * tokens // n_seq)
    slots, blocks = n_seq * cap, width // LANES
    groups, breadth = short_filter.shape[0], down.shape[1]
    packed = pltpu.VMEM((slots * blocks, LANES), BF16)
    spread = pltpu.VMEM((slots, width), BF16)
    vmem = pl.BlockSpec(memory_space=pltpu.VMEM)
    arguments = list(arguments)
    arguments[10] = storage.reshape(1, n_seq)
    arguments[13] = arguments[13].reshape(1, groups)
    outs = (
        jax.ShapeDtypeStruct((tokens, width), BF16),
        jax.ShapeDtypeStruct((tokens, width), BF16),
        jax.ShapeDtypeStruct((1, breadth, width), F32),
        jax.ShapeDtypeStruct((1, breadth, width), F32),
        jax.ShapeDtypeStruct(short_filter.shape, F32),
        jax.ShapeDtypeStruct(medium_filter.shape, F32),
    )
    return pl.pallas_call(
        functools.partial(kernel, n_seq, n_ch, n_y, cap),
        out_shape=outs,
        in_specs=[vmem] * len(arguments),
        out_specs=[vmem] * len(outs),
        scratch_shapes=[
            pltpu.VMEM((slots * blocks, width), BF16),
            pltpu.VMEM((width, slots * blocks), BF16),
            pltpu.VMEM((2 * LANES, 2 * LANES), BF16),
            pltpu.VMEM((groups, tokens, 2 * tokens), BF16),
            pltpu.VMEM((groups, tokens, 2 * tokens), BF16),
            pltpu.VMEM((2 * tokens, width), BF16),
            pltpu.VMEM((tokens + 16, width), BF16),
            pltpu.VMEM((tokens + 16, width), BF16),
            pltpu.VMEM((2 * tokens, width), BF16),
            packed, packed, packed, packed, packed, packed, packed, packed,
            spread, spread,
            pltpu.VMEM((n_ch, breadth, slots), F32),
            pltpu.VMEM((n_ch, breadth, slots), F32),
            pltpu.VMEM((blocks, 16, LANES), F32),
            pltpu.VMEM((n_y, 16, LANES), F32),
            pltpu.VMEM((n_seq // n_y, 16, LANES), F32),
            pltpu.VMEM((n_y, 16, LANES), F32),
            pltpu.VMEM((groups, LANES), F32),
            pltpu.VMEM((groups, LANES), F32),
            pltpu.SemaphoreType.DMA((13,)),
            pltpu.SemaphoreType.DMA((13,)),
        ],
        compiler_params=pltpu.CompilerParams(
            collective_id=0, has_side_effects=True, vmem_limit_bytes=56 * 1024 * 1024
        ),
    )(*arguments)


def solution(mesh):
    tile, factor = P("seq", "ch"), P("seq", None, "ch")
    return jax.shard_map(
        functools.partial(on_device, 4),
        mesh=mesh,
        in_specs=(tile,) * 7
        + (factor, factor, P("seq", None), P(), P("ch", None), P("ch", None), P("ch")),
        out_specs=(tile, tile, factor, factor, P("ch", None), P("ch", None)),
        check_vma=False,
    )
```

time: 735 us -> 107 us (0.15)
  the two profiles are of different devices: /device:TPU:2 before, /device:TPU:1 now
where the time goes in v1:
time: 107 us; the launch traced here: 105 us
  Pallas kernels  96 us (90%)
  local copies, waits for them, and re-layouts  8.16 us (8%)
    pallas_call x1, Pallas kernels, on_device(): pl.pallas_call(functools.partial(kernel, n_seq, n_ch, n_y, cap), out_shap...  96 us
    unnamed x17, local copies, waits for them, and re-layouts  6.77 us

profile of v1, /device:TPU:1, one launch (start us, length us, event | category | flops | bytes accessed | tf_op | source)
XLA Modules:
  0.0 104.9 jit_solution(15395878310138638381)
XLA Ops:
  0.6 0.0 copy-start.4
  0.6 1.4 %copy.21.short_filter = f32[32,7]{1,0:T(8,128)} copy(f32[32,7]{0,1:T(8,128)} %param.25) | data formatting | bytes 1792 | tf_op args[11]
  2.0 0.0 copy-done.4
  2.0 0.7 copy.20.clade
  2.8 96.0 %shard_map.181 = (bf16[128,512]{1,0:T(8,128)(2,1)}, bf16[128,512]{1,0:T(8,128)(2,1)}, f32[1,32,512]{2,1,0:T(8,128)}, f32[1,32,512]{2,1,0:T(8,128)}, f32[32,7]{1,0:T(8,128)}, /*index=5*/f32[32,128]{1,0:T(8,128)}) custom-call(bf16[128,512]{1,0:T(8,128)(2,1)} %x.1, bf16[128,512]{1,0:T(8,128)(2,1)} %soq.1, bf16[128,512]{1,0:T(8,128)(2,1)} %sik.1, ...), custom_call_target="tpu_custom_call" | custom-call | tf_op jit(solution)/shard_map/pallas_call | solution.py:418
  98.8 1.4 %copy.22 = f32[32,7]{0,1:T(8,128)} copy(f32[32,7]{1,0:T(8,128)} %get-tuple-element.10) | data formatting | bytes 1792 | tf_op jit(solution)/shard_map/pallas_call | solution.py:418
  100.2 0.0 copy-start
  100.2 1.6 %copy.28 = bf16[128,512]{1,0:T(8,128)(2,1)} copy(bf16[128,512]{1,0:T(8,128)(2,1)} %get-tuple-element.18) | data formatting | bytes 262144
  101.8 0.0 copy-done
  101.8 0.0 copy-start.2
  101.8 0.7 copy.29
  102.5 0.2 copy-done.2
  102.7 0.0 copy-start.1
  102.7 0.6 copy.30
  103.3 0.2 copy-done.1
  103.5 0.0 copy-start.3
  103.5 0.6 copy.31
  104.2 0.1 copy-done.3
  104.3 0.6 copy.32
Async XLA Ops:
  0.6 1.4 %copy-start.4 = (s32[128,1]{0,1:T(1,128)S(1)}, s32[128,1]{0,1:T(1,128)}, u32[]{:S(2)}) copy-start(s32[128,1]{0,1:T(1,128)} %param.23) | copy-start | bytes 1540
  100.2 1.6 %copy-start = (bf16[128,512]{1,0:T(8,128)(2,1)S(1)}, bf16[128,512]{1,0:T(8,128)(2,1)}, u32[]{:S(2)}) copy-start(bf16[128,512]{1,0:T(8,128)(2,1)} %get-tuple-element.19) | copy-start | bytes 393220
  101.8 0.9 copy-start.2
  102.7 0.9 copy-start.1
  103.5 0.7 copy-start.3

commit v2 on v1

--- a/solution.py
+++ b/solution.py
@@ -47,7 +47,7 @@
 def kernel(
     n_seq, n_ch, n_y, cap,
     x, soq, sik, sfv, moq, mik, cot, down, up, clade, storage, short_filter, medium_filter, rate,
-    response, dx_out, projector, expander, brief, midrange,
+    response, dx_out, projector, expander, sums,
     place, place_t, swap, toep_b, toep_f, mgext, sgext, siext, medext,
     xs, xr, ds, dr, us, ur, es, er, yx, yd, codes_all, cgrad_all, fg, yr, zr, fr, taps, mirror,
     send, recv,
@@ -56,8 +56,7 @@
     blocks = width // LANES
     slots = n_seq * cap
     chunk = blocks * cap
-    groups = short_filter.shape[0]
-    short_len = short_filter.shape[1]
+    short_len, groups = short_filter.shape
     per_block = groups // blocks
     size = width // groups
     n_z = n_seq // n_y
@@ -79,10 +78,14 @@
     def rows_of(ref, device):
         return ref.at[pl.ds(pl.multiple_of(device * chunk, chunk), chunk), :]
 
+    def partner(turn):
+        far = n_seq // 2 - (turn + 1) // 2
+        return lax.rem(me + n_seq + far * (2 * lax.rem(turn, 2) - 1), n_seq)
+
     def exchange(kind, source, target):
-        @pl.loop(1, n_seq)
-        def _(step):
-            peer = lax.rem(me + step, n_seq)
+        @pl.loop(0, n_seq - 1)
+        def _(turn):
+            peer = partner(turn)
             push(kind, rows_of(source, peer), rows_of(target, me), {"seq": peer})
 
         pltpu.make_async_copy(rows_of(source, me), rows_of(target, me), recv.at[kind]).start()
@@ -95,10 +98,10 @@
 
     barrier = pltpu.get_barrier_semaphore()
 
-    @pl.loop(1, n_seq)
-    def _(step):
+    @pl.loop(0, n_seq - 1)
+    def _(turn):
         pl.semaphore_signal(
-            barrier, inc=1, device_id={"seq": lax.rem(me + step, n_seq)}, device_id_type=MESH
+            barrier, inc=1, device_id={"seq": partner(turn)}, device_id_type=MESH
         )
 
     @pl.loop(1, n_ch)
@@ -109,8 +112,8 @@
 
     square = (tokens, tokens)
     eye = iota(square, 0) == iota(square, 1)
-    clade_row = jnp.sum(jnp.where(eye, clade[...], 0).astype(F32), axis=0, keepdims=True)
-    clade_col = clade[...].astype(F32)
+    clade_row = clade[...].astype(F32)
+    clade_col = jnp.sum(jnp.where(eye, clade_row, 0.0), axis=1, keepdims=True)
     earlier = (clade_col == clade_row) & (iota(square, 1) < iota(square, 0))
     rank = jnp.sum(jnp.where(earlier, 1.0, 0.0), axis=1, keepdims=True)
     names = iota((tokens, n_seq), 1).astype(F32)
@@ -128,14 +131,6 @@
     xs[...] = mm(place[...], stacked(x[...])).astype(BF16)
     mgext[0:tokens, :] = (cot[...].astype(F32) * moq[...].astype(F32)).astype(BF16)
 
-    pl.semaphore_wait(barrier, n_seq - 1 + n_ch - 1)
-
-    @pl.when(me > 0)
-    def _():
-        push(MG_HALO, mgext.at[0:tokens, :], mgext.at[tokens : 2 * tokens, :], {"seq": me - 1})
-
-    exchange(X_OUT, xs, xr)
-
     eye_g = iota((groups, groups), 0) == iota((groups, groups), 1)
     rate_col = jnp.sum(jnp.where(eye_g, rate[...], 0.0), axis=1, keepdims=True)
     envelope = jnp.exp(-rate_col * iota((groups, LANES), 1).astype(F32))
@@ -158,8 +153,30 @@
     of_group = jnp.where(
         iota((groups, width), 1) // size == iota((groups, width), 0), 1.0, 0.0
     )
-    short_wide = t_mm(short_filter[...], of_group, lax.Precision.HIGHEST)
+    short_wide = jnp.dot(
+        short_filter[...], of_group, precision=lax.Precision.HIGHEST, preferred_element_type=F32
+    )
     lane_group = iota(square, 1) // size
+
+    for b in range(blocks):
+        place_t[b * tokens : (b + 1) * tokens, :] = jnp.where(
+            iota((tokens, slots * blocks), 1) == key_col + b * cap, 1.0, 0.0
+        ).astype(BF16)
+
+    part = 2 * LANES
+    per_part = part // blocks
+    at = iota((part, part), 0)
+    inside = lax.rem(at, per_part)
+    wanted = (inside // cap) * chunk + (at // per_part) * cap + lax.rem(inside, cap)
+    swap[...] = jnp.where(iota((part, part), 1) == wanted, 1.0, 0.0).astype(BF16)
+
+    pl.semaphore_wait(barrier, n_seq - 1 + n_ch - 1)
+
+    @pl.when(me > 0)
+    def _():
+        push(MG_HALO, mgext.at[0:tokens, :], mgext.at[tokens : 2 * tokens, :], {"seq": me - 1})
+
+    exchange(X_OUT, xs, xr)
 
     def banded(ref, bands, b):
         data = ref[:, lane_block(b)]
@@ -185,13 +202,6 @@
     @pl.when(me > 0)
     def _():
         push(SG_HALO, sgext.at[0:16, :], sgext.at[tokens : tokens + 16, :], {"seq": me - 1})
-
-    part = 2 * LANES
-    per_part = part // blocks
-    at = iota((part, part), 0)
-    inside = lax.rem(at, per_part)
-    wanted = (inside // cap) * chunk + (at // per_part) * cap + lax.rem(inside, cap)
-    swap[...] = jnp.where(iota((part, part), 1) == wanted, 1.0, 0.0).astype(BF16)
 
     def opened(packed, target):
         for p in range(slots // per_part):
@@ -237,11 +247,6 @@
     codes = summed(codes_all).astype(BF16)
     closed((0.5 * t_mm(codes, up[0])).astype(BF16), us)
     exchange(DELTA_BACK, us, ur)
-
-    for b in range(blocks):
-        place_t[b * tokens : (b + 1) * tokens, :] = jnp.where(
-            iota((tokens, slots * blocks), 1) == key_col + b * cap, 1.0, 0.0
-        ).astype(BF16)
 
     weight_scale = 1.0 / math.sqrt(tokens)
     landed(DG_OUT, dr)
@@ -385,12 +390,32 @@
 
     landed(SPREAD_Y, fr.at[0 : n_y - 1])
     gone(SPREAD_Y, fr.at[0 : n_y - 1])
-    filter_scale = 1.0 / math.sqrt(tokens * n_seq * size)
+    sums[...] = fr[...]
+
+
+def finish(
+    n_seq, response, dx, projector, expander, sums, rate,
+    response_out, dx_out, projector_out, expander_out, brief, midrange,
+):
+    tokens, width = response.shape
+    short_len, groups = brief.shape
+    blocks, per_block, size = sums.shape[0], groups // sums.shape[0], width // groups
+    response_out[...] = response[...]
+    dx_out[...] = dx[...]
+    projector_out[...] = projector[...]
+    expander_out[...] = expander[...]
+    eye = iota((groups, groups), 0) == iota((groups, groups), 1)
+    rate_col = jnp.sum(jnp.where(eye, rate[...], 0.0), axis=1, keepdims=True)
+    envelope = jnp.exp(-rate_col * iota((groups, LANES), 1).astype(F32))
+    scale = 1.0 / math.sqrt(tokens * n_seq * size)
     for b in range(blocks):
         rows = slice(b * per_block, (b + 1) * per_block)
-        midrange[rows, :] = fr[b, 0:8, :] * (envelope[rows] * filter_scale)
-    lines = jnp.concatenate([fr[b, 8:16, :] for b in range(blocks)], axis=1)
-    brief[...] = mm_t(of_group, lines, lax.Precision.HIGHEST)[:, 0:short_len] * filter_scale
+        midrange[rows, :] = sums[b, 0:8, :] * (envelope[rows] * scale)
+    of_group = jnp.where(
+        iota((groups, width), 1) // size == iota((groups, width), 0), 1.0, 0.0
+    )
+    lines = jnp.concatenate([sums[b, 8:16, :] for b in range(blocks)], axis=1)
+    brief[...] = mm_t(lines, of_group, lax.Precision.HIGHEST)[0:short_len] * scale
 
 
 def on_device(n_y, *arguments):
@@ -405,21 +430,25 @@
     spread = pltpu.VMEM((slots, width), BF16)
     vmem = pl.BlockSpec(memory_space=pltpu.VMEM)
     arguments = list(arguments)
+    arguments[9] = arguments[9].T
     arguments[10] = storage.reshape(1, n_seq)
+    arguments[11] = short_filter.T
     arguments[13] = arguments[13].reshape(1, groups)
     outs = (
         jax.ShapeDtypeStruct((tokens, width), BF16),
         jax.ShapeDtypeStruct((tokens, width), BF16),
         jax.ShapeDtypeStruct((1, breadth, width), F32),
         jax.ShapeDtypeStruct((1, breadth, width), F32),
-        jax.ShapeDtypeStruct(short_filter.shape, F32),
+    )
+    filters = (
+        jax.ShapeDtypeStruct(short_filter.shape[::-1], F32),
         jax.ShapeDtypeStruct(medium_filter.shape, F32),
     )
-    return pl.pallas_call(
+    results = pl.pallas_call(
         functools.partial(kernel, n_seq, n_ch, n_y, cap),
-        out_shape=outs,
+        out_shape=outs + (jax.ShapeDtypeStruct((blocks, 16, LANES), F32),),
         in_specs=[vmem] * len(arguments),
-        out_specs=[vmem] * len(outs),
+        out_specs=[vmem] * (len(outs) + 1),
         scratch_shapes=[
             pltpu.VMEM((slots * blocks, width), BF16),
             pltpu.VMEM((width, slots * blocks), BF16),
@@ -447,6 +476,13 @@
             collective_id=0, has_side_effects=True, vmem_limit_bytes=56 * 1024 * 1024
         ),
     )(*arguments)
+    *results, brief, midrange = pl.pallas_call(
+        functools.partial(finish, n_seq),
+        out_shape=outs + filters,
+        in_specs=[vmem] * 6,
+        out_specs=[vmem] * 6,
+    )(*results, arguments[13])
+    return (*results, brief.T, midrange)
 
 
 def solution(mesh):

time: 107 us -> 98.9 us (0.924)
  the two profiles are of different devices: /device:TPU:1 before, /device:TPU:2 now
where the time goes in v2:
time: 98.9 us; the launch traced here: 98.7 us
  Pallas kernels  98.1 us (99%)
    pallas_call x1, Pallas kernels, on_device(): pl.pallas_call(functools.partial(kernel, n_seq, n_ch, n_y, cap), out_shap...  96.2 us

profile of v2, /device:TPU:2, one launch (start us, length us, event | category | flops | bytes accessed | tf_op | source)
XLA Modules:
  0.0 98.7 jit_solution(2918430831544837154)
XLA Ops:
  0.6 96.2 %shard_map.181 = (bf16[128,512]{1,0:T(8,128)(2,1)}, bf16[128,512]{1,0:T(8,128)(2,1)}, f32[1,32,512]{2,1,0:T(8,128)}, f32[1,32,512]{2,1,0:T(8,128)}, f32[4,16,128]{2,1,0:T(8,128)}) custom-call(bf16[128,512]{1,0:T(8,128)(2,1)} %x.1, bf16[128,512]{1,0:T(8,128)(2,1)} %soq.1, bf16[128,512]{1,0:T(8,128)(2,1)} %sik.1, bf16[128,512]{1,0:T(8,128)(2,1)} %sfv.1, ...), custom_call_target="tpu_custom_call" | custom-call | tf_op jit(solution)/shard_map/pallas_call | solution.py:447
  96.9 1.9 %shard_map.182 = (bf16[128,512]{1,0:T(8,128)(2,1)}, bf16[128,512]{1,0:T(8,128)(2,1)}, f32[1,32,512]{2,1,0:T(8,128)}, f32[1,32,512]{2,1,0:T(8,128)}, f32[7,32]{1,0:T(8,128)}, /*index=5*/f32[32,128]{1,0:T(8,128)}) custom-call(bf16[128,512]{1,0:T(8,128)(2,1)} %get-tuple-element.17.response, bf16[128,512]{1,0:T(8,128)(2,1)} %get-tuple-element.18.dx, ...), custom_call_target="tpu_custom_call" | custom-call | tf_op jit(solution)/shard_map/pallas_call | solution.py:479

commit v3 on v2

--- a/solution.py
+++ b/solution.py
@@ -82,13 +82,14 @@
         far = n_seq // 2 - (turn + 1) // 2
         return lax.rem(me + n_seq + far * (2 * lax.rem(turn, 2) - 1), n_seq)
 
-    def exchange(kind, source, target):
-        @pl.loop(0, n_seq - 1)
+    def exchange(kind, source, target, first=0, last=n_seq - 1):
+        @pl.loop(first, last)
         def _(turn):
             peer = partner(turn)
             push(kind, rows_of(source, peer), rows_of(target, me), {"seq": peer})
 
-        pltpu.make_async_copy(rows_of(source, me), rows_of(target, me), recv.at[kind]).start()
+        if last == n_seq - 1:
+            pltpu.make_async_copy(rows_of(source, me), rows_of(target, me), recv.at[kind]).start()
 
     def share(kind, ref):
         @pl.loop(1, n_ch)
@@ -235,7 +236,8 @@
         total = total + short_wide[j : j + 1, :] * ahead[j : j + tokens]
     delta_grad = (0.5 * total * sik[...].astype(F32)).astype(BF16)
     ds[...] = mm(place[...], stacked(delta_grad)).astype(BF16)
-    exchange(DG_OUT, ds, dr)
+    split = 3 * n_seq // 8
+    exchange(DG_OUT, ds, dr, first=split)
 
     def summed(ref):
         total = ref[0]
@@ -247,13 +249,7 @@
     codes = summed(codes_all).astype(BF16)
     closed((0.5 * t_mm(codes, up[0])).astype(BF16), us)
     exchange(DELTA_BACK, us, ur)
-
-    weight_scale = 1.0 / math.sqrt(tokens)
-    landed(DG_OUT, dr)
-    opened(dr, yd)
-    cgrad_all[mine] = mm_t(up[0], yd[...])
-    share(CODES_GRAD, cgrad_all)
-    expander[0] = mm(codes, yd[...]) * weight_scale
+    exchange(DG_OUT, ds, dr, last=split)
 
     landed(DELTA_BACK, ur)
     delta = mm(place_t[...], ur[...]).astype(BF16).astype(F32)
@@ -268,11 +264,6 @@
     def _():
         push(SI_HALO, siext.at[tokens : tokens + 16, :], siext.at[0:16, :], {"seq": me + 1})
 
-    landed(CODES_GRAD, cgrad_all.at[0 : n_ch - 1])
-    codes_grad = summed(cgrad_all).astype(BF16)
-    closed(t_mm(codes_grad, down[0]).astype(BF16), es)
-    exchange(DX_BACK, es, er)
-
     @pl.when(me > 0)
     def _():
         landed(SI_HALO, siext.at[0:16, :])
@@ -291,7 +282,6 @@
     def _():
         push(MED_HALO, medext.at[0:tokens, :], medext.at[tokens : 2 * tokens, :], {"seq": me + 1})
 
-    projector[0] = mm(codes_grad, yx[...]) * weight_scale
     short_grad = sgext[0:tokens, :].astype(F32)
     fg[:, 8:16, :] = jnp.zeros((blocks, 8, LANES), F32)
     for j in range(short_len):
@@ -342,6 +332,11 @@
             banded(medext, toep_f, b) * moq[:, lanes].astype(F32)
         ).astype(BF16)
 
+    landed(DG_OUT, dr)
+    opened(dr, yd)
+    cgrad_all[mine] = mm_t(up[0], yd[...])
+    share(CODES_GRAD, cgrad_all)
+
     @pl.loop(0, blocks // 2)
     def _(b):
         respond(b)
@@ -354,22 +349,31 @@
         peer = lax.rem(my_z + step, n_z)
         push(SUM_Z, zr.at[my_z], zr.at[my_z], {"seq": peer * n_y + my_y})
 
+    landed(CODES_GRAD, cgrad_all.at[0 : n_ch - 1])
+    codes_grad = summed(cgrad_all).astype(BF16)
+    closed(t_mm(codes_grad, down[0]).astype(BF16), es)
+    exchange(DX_BACK, es, er)
+
     @pl.loop(blocks // 2, blocks)
     def _(b):
         respond(b)
+
+    landed(SUM_Z, zr.at[0 : n_z - 1])
+    fr[my_y] = summed(zr)
+
+    @pl.loop(1, n_y)
+    def _(step):
+        peer = lax.rem(my_y + step, n_y)
+        push(SPREAD_Y, fr.at[my_y], fr.at[my_y], {"seq": my_z * n_y + peer})
+
+    weight_scale = 1.0 / math.sqrt(tokens)
+    expander[0] = mm(codes, yd[...]) * weight_scale
+    projector[0] = mm(codes_grad, yx[...]) * weight_scale
 
     landed(DX_BACK, er)
     back = mm(place_t[...], er[...]).astype(BF16)
     for b in range(blocks):
         dx_out[:, b * LANES : (b + 1) * LANES] = back[b * tokens : (b + 1) * tokens]
-
-    landed(SUM_Z, zr.at[0 : n_z - 1])
-    fr[my_y] = summed(zr)
-
-    @pl.loop(1, n_y)
-    def _(step):
-        peer = lax.rem(my_y + step, n_y)
-        push(SPREAD_Y, fr.at[my_y], fr.at[my_y], {"seq": my_z * n_y + peer})
 
     @pl.when(me > 0)
     def _():

time: 98.9 us -> 98 us (level)
  the two profiles are of different devices: /device:TPU:2 before, /device:TPU:1 now
where the time goes in v3:
time: 98 us; the launch traced here: 97.9 us
  Pallas kernels  97.2 us (99%)
    pallas_call x1, Pallas kernels, on_device(): pl.pallas_call(functools.partial(kernel, n_seq, n_ch, n_y, cap), out_shap...  95.4 us

profile of v3, /device:TPU:1, one launch (start us, length us, event | category | flops | bytes accessed | tf_op | source)
XLA Modules:
  0.0 97.9 jit_solution(17068974792976877581)
XLA Ops:
  0.6 95.4 %shard_map.181 = (bf16[128,512]{1,0:T(8,128)(2,1)}, bf16[128,512]{1,0:T(8,128)(2,1)}, f32[1,32,512]{2,1,0:T(8,128)}, f32[1,32,512]{2,1,0:T(8,128)}, f32[4,16,128]{2,1,0:T(8,128)}) custom-call(bf16[128,512]{1,0:T(8,128)(2,1)} %x.1, bf16[128,512]{1,0:T(8,128)(2,1)} %soq.1, bf16[128,512]{1,0:T(8,128)(2,1)} %sik.1, bf16[128,512]{1,0:T(8,128)(2,1)} %sfv.1, ...), custom_call_target="tpu_custom_call" | custom-call | tf_op jit(solution)/shard_map/pallas_call | solution.py:451
  96.0 1.9 %shard_map.182 = (bf16[128,512]{1,0:T(8,128)(2,1)}, bf16[128,512]{1,0:T(8,128)(2,1)}, f32[1,32,512]{2,1,0:T(8,128)}, f32[1,32,512]{2,1,0:T(8,128)}, f32[7,32]{1,0:T(8,128)}, /*index=5*/f32[32,128]{1,0:T(8,128)}) custom-call(bf16[128,512]{1,0:T(8,128)(2,1)} %get-tuple-element.17.response, bf16[128,512]{1,0:T(8,128)(2,1)} %get-tuple-element.18.dx, ...), custom_call_target="tpu_custom_call" | custom-call | tf_op jit(solution)/shard_map/pallas_call | solution.py:483

commit v4 on v3

--- a/solution.py
+++ b/solution.py
@@ -281,6 +281,11 @@
     @pl.when(me < n_seq - 1)
     def _():
         push(MED_HALO, medext.at[0:tokens, :], medext.at[tokens : 2 * tokens, :], {"seq": me + 1})
+
+    landed(DG_OUT, dr)
+    opened(dr, yd)
+    cgrad_all[mine] = mm_t(up[0], yd[...])
+    share(CODES_GRAD, cgrad_all)
 
     short_grad = sgext[0:tokens, :].astype(F32)
     fg[:, 8:16, :] = jnp.zeros((blocks, 8, LANES), F32)
@@ -332,10 +337,10 @@
             banded(medext, toep_f, b) * moq[:, lanes].astype(F32)
         ).astype(BF16)
 
-    landed(DG_OUT, dr)
-    opened(dr, yd)
-    cgrad_all[mine] = mm_t(up[0], yd[...])
-    share(CODES_GRAD, cgrad_all)
+    landed(CODES_GRAD, cgrad_all.at[0 : n_ch - 1])
+    codes_grad = summed(cgrad_all).astype(BF16)
+    closed(t_mm(codes_grad, down[0]).astype(BF16), es)
+    exchange(DX_BACK, es, er)
 
     @pl.loop(0, blocks // 2)
     def _(b):
@@ -348,11 +353,6 @@
     def _(step):
         peer = lax.rem(my_z + step, n_z)
         push(SUM_Z, zr.at[my_z], zr.at[my_z], {"seq": peer * n_y + my_y})
-
-    landed(CODES_GRAD, cgrad_all.at[0 : n_ch - 1])
-    codes_grad = summed(cgrad_all).astype(BF16)
-    closed(t_mm(codes_grad, down[0]).astype(BF16), es)
-    exchange(DX_BACK, es, er)
 
     @pl.loop(blocks // 2, blocks)
     def _(b):

time: 98 us -> 101 us (1.031)
  Pallas kernels: 97.2 us -> 101 us
    pallas_call x1, Pallas kernels: 95.4 us -> 98.8 us  [on_device(): pl.pallas_call(functools.partial(kernel, n_seq, n_ch, n_y, cap), out_shap...]
where the time goes in v4:
time: 101 us
  Pallas kernels  101 us (100%)
    pallas_call x1, Pallas kernels, on_device(): pl.pallas_call(functools.partial(kernel, n_seq, n_ch, n_y, cap), out_shap...  98.8 us

profile of v4, /device:TPU:1, one launch (start us, length us, event | category | flops | bytes accessed | tf_op | source)
XLA Modules:
  0.0 101.3 jit_solution(13742857048224301667)
XLA Ops:
  0.6 98.8 %shard_map.181 = (bf16[128,512]{1,0:T(8,128)(2,1)}, bf16[128,512]{1,0:T(8,128)(2,1)}, f32[1,32,512]{2,1,0:T(8,128)}, f32[1,32,512]{2,1,0:T(8,128)}, f32[4,16,128]{2,1,0:T(8,128)}) custom-call(bf16[128,512]{1,0:T(8,128)(2,1)} %x.1, bf16[128,512]{1,0:T(8,128)(2,1)} %soq.1, bf16[128,512]{1,0:T(8,128)(2,1)} %sik.1, bf16[128,512]{1,0:T(8,128)(2,1)} %sfv.1, ...), custom_call_target="tpu_custom_call" | custom-call | tf_op jit(solution)/shard_map/pallas_call | solution.py:451
  99.4 1.9 %shard_map.182 = (bf16[128,512]{1,0:T(8,128)(2,1)}, bf16[128,512]{1,0:T(8,128)(2,1)}, f32[1,32,512]{2,1,0:T(8,128)}, f32[1,32,512]{2,1,0:T(8,128)}, f32[7,32]{1,0:T(8,128)}, /*index=5*/f32[32,128]{1,0:T(8,128)}) custom-call(bf16[128,512]{1,0:T(8,128)(2,1)} %get-tuple-element.17.response, bf16[128,512]{1,0:T(8,128)(2,1)} %get-tuple-element.18.dx, ...), custom_call_target="tpu_custom_call" | custom-call | tf_op jit(solution)/shard_map/pallas_call | solution.py:483
